TPU v7x, 256 devices: a whole 4x4x8 slice. The times are simulated.
256 devices in a mesh: row: 32 (over z, y_lo, core), col: 8 (over y_hi, x).
Axes of the slice: x: 4, y: 4 (y_hi: 2, y_lo: 2; y = y_hi * 2 + y_lo), z: 8, core: 2. Of those that a mesh axis runs over, the one named last changes fastest.
Arguments:
- matrix: float32 [14336, 14336], P('row', 'col'), may hold values from -16 to 16, as said below
- panels: float32 [2, 14336, 128], P(None, 'row'), may hold values from -0.050111484 to 0.050111484
- factors: float32 [2, 128, 128], replicated, may hold values from -1.2 to 1.6, as said below
Outputs:
- updated: float32 [14336, 14336], P('row', 'col')
Inputs may be any that keep to these rules, and one draw needn't show every extreme that they name: symmetric: matrix[r, c] equals matrix[c, r]. Each factors[p] is upper triangular, with diagonal entries between 0.8 and 1.6.
All inputs are finite; a program needn't handle non-finite values.
Results may differ from a plain program's by a relative error of at most 0.0001.
Values sent between devices are 32-bit elements; how exact they have to be, the bound alone decides.
A program may use at most 64 MiB of HBM per device.

v0:
```python
import jax
import jax.numpy as jnp
from jax import lax
from jax.sharding import PartitionSpec as P


def matmul(former, latter):
    return jnp.dot(former, latter, precision=lax.Precision.HIGHEST)


def transposed_dot(former, latter):
    return lax.dot_general(
        former, latter, (((0,), (0,)), ((), ())), precision=lax.Precision.HIGHEST
    )


def outer_drop(current, former, latter):
    return current - lax.dot_general(
        former, latter, (((1,), (1,)), ((), ())), precision=lax.Precision.HIGHEST
    )


def weights(forward, vectors, factor, correct):
    return matmul(forward, factor) - 0.5 * matmul(vectors, correct)


def row_sums(current, vector_rows, extra_terms):
    summed = lax.psum((transposed_dot(current, vector_rows),) + extra_terms, "row")
    return (summed[0], tuple(summed[1:]))


def shards(matrix, panels, factors):
    col_index = lax.axis_index("col")
    local_cols = matrix.shape[1]
    gathered = lax.all_gather(panels, "row", axis=1, tiled=True)
    vector_cols = lax.dynamic_slice_in_dim(gathered, col_index * local_cols, local_cols, 1)
    current = matrix
    for number in range(panels.shape[0]):
        vector_rows = panels[number]
        vcol_now = vector_cols[number]
        factor = factors[number]
        forward = lax.psum(matmul(current, vcol_now), "col")
        forward_cols, summed = row_sums(
            current, vector_rows, (transposed_dot(vector_rows, forward),)
        )
        correct = matmul(factor.T, matmul(summed[0], factor))
        wrow_now = weights(forward, vector_rows, factor, correct)
        wcol_now = weights(forward_cols, vcol_now, factor, correct)
        current = outer_drop(
            current,
            jnp.concatenate([vector_rows, wrow_now], axis=1),
            jnp.concatenate([wcol_now, vcol_now], axis=1),
        )
    return current


def solution(mesh):
    placed = (P("row", "col"), P(None, "row", None), P())
    return jax.shard_map(
        shards, mesh=mesh, in_specs=placed, out_specs=P("row", "col"), check_vma=False
    )
```

profile of v0, /device:TPU:1, one launch (start us, length us, event | category | flops | bytes accessed | tf_op | source)
XLA Modules:
  0.0 775.0 jit_solution(1958344349460214117)
XLA Ops:
  6.5 0.0 copy-start
  6.5 0.0 all-gather.2.cloned.1.call-start
  6.5 0.7 all-gather.2.cloned.1.call-update
  7.3 0.0 all-reduce.7.cloned.1.call-start
  7.3 95.2 %all-gather.2.cloned.1.call-done = f32[2,14336,128]{2,1,0:T(8,128)} async-done(((f32[2,448,128]{2,1,0:T(8,128)}), f32[2,14336,128]{2,1,0:T(8,128)}) %all-gather.2.cloned.1.call-update) | async-done | bytes 14680080 | tf_op jit(solution)/shard_map/all_gather | solution.py:35
  102.5 2.5 dynamic-slice_bitcast_fusion
  105.0 0.0 copy-start.3
  105.0 0.9 copy-done.3
  105.9 0.0 copy-done
  105.9 3.4 convolution_bitcast_fusion
  109.3 0.0 all-reduce.7.cloned.1.call-update
  109.3 0.0 copy-start.7
  109.3 0.0 all-reduce.13.cloned.1.call-start
  109.4 7.8 %fusion.44 = f32[1792,128]{1,0:T(8,128)} fusion(f32[448,1792]{1,0:T(8,128)S(1)} %copy-done, f32[2,448,128]{2,1,0:T(8,128)} %param.4), kind=kOutput, calls=%fused_computation.57 | convolution fusion | flops 1233125376 | bytes 4358144 | tf_op jit(solution)/shard_map/dot_general | solution.py:12
  117.2 0.0 copy-start.4
  117.2 74.7 %all-reduce.7.cloned.1.call-done = f32[448,128]{1,0:T(8,128)} async-done(((f32[448,128]{1,0:T(8,128)}), f32[448,128]{1,0:T(8,128)}) %all-reduce.7.cloned.1.call-update) | async-done | bytes 229392 | tf_op jit(solution)/shard_map/psum | solution.py:42
  191.9 2.3 convolution_bitcast_fusion.2
  194.1 0.0 all-reduce.13.cloned.1.call-update
  194.2 0.0 copy-start.5
  194.2 0.2 all-reduce.9.cloned.1.call-start
  194.4 1.9 slice_bitcast_fusion
  196.3 0.0 copy-done.7
  196.3 1.3 fusion.32
  197.6 228.8 %all-reduce.13.cloned.1.call-done = (f32[1792,128]{1,0:T(8,128)}, f32[128,128]{0,1:T(8,128)}) async-done(((f32[1792,128]{1,0:T(8,128)}, f32[128,128]{0,1:T(8,128)}), (f32[1792,128]{1,0:T(8,128)}, f32[128,128]{0,1:T(8,128)})) %all-reduce.13.cloned.1.call-update) | async-done | bytes 983056 | tf_op jit(solution)/shard_map/psum | solution.py:28
  426.3 0.0 copy-start.9
  426.3 2.1 fusion.26
  428.4 1.1 fusion.30
  429.6 0.3 fusion.28
  429.9 0.0 copy-done.4
  429.9 0.9 fusion.1
  430.8 0.0 copy-done.5
  430.8 0.4 fusion.11
  431.1 0.0 copy-done.9
  431.2 0.0 copy-start.1
  431.2 5.1 convolution_subtract_fusion.1
  436.3 0.0 copy-done.1
  436.3 3.4 fusion.46
  439.6 0.0 all-reduce.9.cloned.1.call-update
  439.7 0.3 all-reduce.11.cloned.1.call-start
  439.9 7.8 %fusion.45 = f32[1792,128]{1,0:T(8,128)} fusion(f32[448,1792]{1,0:T(8,128)S(1)} %convolution_subtract_fusion.1, f32[2,448,128]{2,1,0:T(8,128)} %param.4), kind=kOutput, calls=%fused_computation.58 | convolution fusion | flops 1233125376 | bytes 4358144 | tf_op jit(solution)/shard_map/dot_general | solution.py:12
  447.7 75.9 %all-reduce.9.cloned.1.call-done = f32[448,128]{1,0:T(8,128)} async-done(((f32[448,128]{1,0:T(8,128)}), f32[448,128]{1,0:T(8,128)}) %all-reduce.9.cloned.1.call-update) | async-done | bytes 229392 | tf_op jit(solution)/shard_map/psum | solution.py:42
  523.6 2.3 convolution_bitcast_fusion.1
  525.9 0.0 all-reduce.11.cloned.1.call-update
  525.9 2.0 fusion.24
  527.9 230.0 %all-reduce.11.cloned.1.call-done = (f32[1792,128]{1,0:T(8,128)}, f32[128,128]{0,1:T(8,128)}) async-done(((f32[1792,128]{1,0:T(8,128)}, f32[128,128]{0,1:T(8,128)}), (f32[1792,128]{1,0:T(8,128)}, f32[128,128]{0,1:T(8,128)})) %all-reduce.11.cloned.1.call-update) | async-done | bytes 983056 | tf_op jit(solution)/shard_map/psum | solution.py:28
  757.9 0.0 copy-start.6
  757.9 0.0 copy-start.10
  757.9 0.0 copy-start.2
  757.9 0.0 copy-start.8
  757.9 2.2 fusion.18
  760.1 1.1 fusion.22
  761.2 0.3 fusion.20
  761.5 2.1 fusion
  763.6 0.0 copy-done.6
  763.6 0.0 copy-done.10
  763.6 0.4 fusion.9
  764.0 0.0 copy-done.2
  764.0 0.0 copy-done.8
  764.0 4.5 convolution_subtract_fusion
Async XLA Ops:
  6.5 99.4 %copy-start = (f32[448,1792]{1,0:T(8,128)S(1)}, f32[448,1792]{1,0:T(8,128)}, u32[]{:S(2)}) copy-start(f32[448,1792]{1,0:T(8,128)} %param.3) | copy-start | bytes 9633796
  6.5 96.0 %all-gather.2.cloned.1.call-start = ((), (), s32[]{:S(2)}) async-start(), calls=%async_computation | async-start | bytes 15138816 | tf_op jit(solution)/shard_map/all_gather | solution.py:35
  7.3 184.6 %all-reduce.7.cloned.1.call-start = ((), (), s32[]{:S(2)}) async-start(), calls=%async_computation.1 | async-start | bytes 458752 | tf_op jit(solution)/shard_map/psum | solution.py:42
  105.0 0.9 copy-start.3
  109.3 87.0 %copy-start.7 = (f32[2,128,128]{2,1,0:T(8,128)S(1)}, f32[2,128,128]{2,1,0:T(8,128)}, u32[]{:S(2)}) copy-start(f32[2,128,128]{2,1,0:T(8,128)} %param.5) | copy-start | bytes 393220
  109.3 317.0 %all-reduce.13.cloned.1.call-start = ((), (), s32[]{:S(2)}) async-start(), calls=%async_computation.4 | async-start | bytes 1966080 | tf_op jit(solution)/shard_map/psum | solution.py:28
  117.2 312.7 %copy-start.4 = (f32[1792,128]{1,0:T(8,128)S(1)}, f32[1792,128]{1,0:T(8,128)}, u32[]{:S(2)}) copy-start(f32[1792,128]{1,0:T(8,128)} %copy-done.3) | copy-start | bytes 2752516
  194.2 236.6 %copy-start.5 = (f32[2,448,128]{2,1,0:T(8,128)S(1)}, f32[2,448,128]{2,1,0:T(8,128)}, u32[]{:S(2)}) copy-start(f32[2,448,128]{2,1,0:T(8,128)} %param.4) | copy-start | bytes 1376260
  194.2 329.4 %all-reduce.9.cloned.1.call-start = ((), (), s32[]{:S(2)}) async-start(), calls=%async_computation.2 | async-start | bytes 458752 | tf_op jit(solution)/shard_map/psum | solution.py:42
  426.3 4.8 copy-start.9
  431.2 5.1 copy-start.1
  439.7 318.2 %all-reduce.11.cloned.1.call-start = ((), (), s32[]{:S(2)}) async-start(), calls=%async_computation.3 | async-start | bytes 1966080 | tf_op jit(solution)/shard_map/psum | solution.py:28
  757.9 5.7 copy-start.6
  757.9 5.7 copy-start.10
  757.9 6.1 copy-start.2
  757.9 6.1 copy-start.8
Sparse Core Ops, SparseCore 0:
  9.1 93.3 all-gather.1
  109.4 82.4 all-reduce.6
  194.6 231.7 all-reduce.12
  439.8 83.7 all-reduce.8
  526.2 231.7 all-reduce.10
where the time goes:
time: 775 us
  waiting for transfers between devices  705 us (91%)
  matrix products  50.4 us (7%)
  between operations  13.3 us (2%)
    psum x2, waiting for transfers between devices, row_sums(): lax.psum((transposed_dot(current, vector_rows),) + extra_terms, 'row')  459 us
    psum x2, waiting for transfers between devices, shards(): forward = lax.psum(matmul(current, vcol_now), 'col')  151 us
    all_gather x1, waiting for transfers between devices, shards(): gathered = lax.all_gather(panels, 'row', axis=1, tiled=True)  95.2 us
    dot_general x14, matrix products, matmul(): return jnp.dot(former, latter, precision=lax.Precision.HIGHEST)  20.8 us
    dot_general x4, matrix products, transposed_dot(): lax.dot_general(former, latter, (((0,), (0,)), ((), ())), precision=lax.P...  20.1 us
  transfers between devices with their start and end apart: 5, of which 5 were waited for; matrix products, arithmetic and copies ran while one was open for 3% of the time, Pallas kernels for 0%

commit v1 on v0

--- a/solution.py
+++ b/solution.py
@@ -30,9 +30,17 @@
 
 
 def shards(matrix, panels, factors):
+
+    def choose_the_chains(work_x, axis_id):
+        series = []
+        for _ in range(lax.axis_size(axis_id)):
+            series.append(work_x)
+        s_next = jnp.concatenate(lax.all_to_all(jnp.stack(series, axis=0), axis_id, 0, 0), axis=1)
+        return s_next
+
     col_index = lax.axis_index("col")
     local_cols = matrix.shape[1]
-    gathered = lax.all_gather(panels, "row", axis=1, tiled=True)
+    gathered = choose_the_chains(panels, "row")
     vector_cols = lax.dynamic_slice_in_dim(gathered, col_index * local_cols, local_cols, 1)
     current = matrix
     for number in range(panels.shape[0]):

time: 775 us -> 1030 us (1.33)
  waiting for transfers between devices: 705 us -> 923 us
  local copies, waits for them, and re-layouts: 5.37 us -> 30.4 us
  starting transfers between devices: 0.57 us -> 12 us
    all_to_all x0 -> x1, waiting for transfers between devices: none -> 314 us  [choose_the_chains(): lax.all_to_all(jnp.stack(series, axis=0), axis_id, 0, 0)]
    all_gather x1 -> x0, waiting for transfers between devices: 95.2 us -> none  [shards(): gathered = lax.all_gather(panels, 'row', axis=1, tiled=True)]
    all_to_all x0 -> x1, local copies, waits for them, and re-layouts: none -> 12.1 us  [choose_the_chains(): lax.all_to_all(jnp.stack(series, axis=0), axis_id, 0, 0)]
    all_to_all x0 -> x1, starting transfers between devices: none -> 11.2 us  [choose_the_chains(): lax.all_to_all(jnp.stack(series, axis=0), axis_id, 0, 0)]
  transfers between devices with their start and end apart: 5 -> 5, of which waited for: 5 -> 5; matrix products, arithmetic and copies ran while one was open for 3% -> 2% of each run, Pallas kernels for 0% -> 0%
where the time goes in v1:
time: 1030 us
  waiting for transfers between devices  923 us (90%)
  matrix products  49.6 us (5%)
  local copies, waits for them, and re-layouts  30.4 us (3%)
  between operations  13.3 us (1%)
  starting transfers between devices  12 us (1%)
    psum x2, waiting for transfers between devices, row_sums(): lax.psum((transposed_dot(current, vector_rows),) + extra_terms, 'row')  455 us
    all_to_all x1, waiting for transfers between devices, choose_the_chains(): lax.all_to_all(jnp.stack(series, axis=0), axis_id, 0, 0)  314 us
    psum x2, waiting for transfers between devices, shards(): forward = lax.psum(matmul(current, vcol_now), 'col')  154 us
  transfers between devices with their start and end apart: 5, of which 5 were waited for; matrix products, arithmetic and copies ran while one was open for 2% of the time, Pallas kernels for 0%

profile of v1, /device:TPU:1, one launch (start us, length us, event | category | flops | bytes accessed | tf_op | source)
XLA Modules:
  0.0 1028.3 jit_solution(12618700984440820401)
XLA Ops:
  6.5 8.0 stack.2
  14.5 11.2 %all-to-all-start = ((f32[32,2,448,128]{3,2,1,0:T(8,128)}), f32[32,2,448,128]{3,2,1,0:T(8,128)}, u32[]{:S(2)}, u32[]{:S(2)}) async-start(f32[32,2,448,128]{3,2,1,0:T(8,128)} %stack.2), calls=%async_computation | async-start | bytes 29360128 | tf_op jit(solution)/shard_map/all_to_all | solution.py:38
  25.7 0.0 all-reduce.7.cloned.1.call-start
  25.7 314.2 %all-to-all-done = f32[32,2,448,128]{3,2,1,0:T(8,128)} async-done(((f32[32,2,448,128]{3,2,1,0:T(8,128)}), f32[32,2,448,128]{3,2,1,0:T(8,128)}, u32[]{:S(2)}, u32[]{:S(2)}) %all-to-all-start) | async-done | bytes 14680096 | tf_op jit(solution)/shard_map/all_to_all | solution.py:38
  340.0 12.1 %copy.4 = f32[32,2,448,128]{3,2,0,1:T(8,128)} copy(f32[32,2,448,128]{3,2,1,0:T(8,128)} %all-to-all-done) | data formatting | bytes 29360128 | tf_op jit(solution)/shard_map/all_to_all | solution.py:38
  352.0 0.0 copy-start
  352.1 2.6 constant_dynamic-slice_fusion.1
  354.7 0.0 copy-start.2
  354.7 0.9 copy-done.2
  355.6 0.0 copy-done
  355.6 3.4 convolution_bitcast_fusion
  359.0 0.0 all-reduce.7.cloned.1.call-update
  359.0 0.2 all-reduce.13.cloned.1.call-start
  359.2 7.8 fusion.49
  367.0 0.0 copy-start.8
  367.0 77.9 %all-reduce.7.cloned.1.call-done = f32[448,128]{1,0:T(8,128)} async-done(((f32[448,128]{1,0:T(8,128)}), f32[448,128]{1,0:T(8,128)}) %all-reduce.7.cloned.1.call-update) | async-done | bytes 229392 | tf_op jit(solution)/shard_map/psum | solution.py:50
  445.0 0.0 copy-start.10
  445.0 2.3 convolution_bitcast_fusion.2
  447.3 0.0 copy-start.3
  447.3 0.0 all-reduce.13.cloned.1.call-update
  447.3 0.3 all-reduce.9.cloned.1.call-start
  447.6 1.9 slice_bitcast_fusion
  449.4 2.4 copy.7
  451.9 0.0 copy-done.8
  451.9 0.0 copy-done.10
  451.9 0.0 copy-start.4
  451.9 0.3 fusion.37
  452.2 227.2 %all-reduce.13.cloned.1.call-done = (f32[1792,128]{1,0:T(8,128)}, f32[128,128]{0,1:T(8,128)}) async-done(((f32[1792,128]{1,0:T(8,128)}, f32[128,128]{0,1:T(8,128)}), (f32[1792,128]{1,0:T(8,128)}, f32[128,128]{0,1:T(8,128)})) %all-reduce.13.cloned.1.call-update) | async-done | bytes 983056 | tf_op jit(solution)/shard_map/psum | solution.py:28
  679.4 0.0 copy-start.7
  679.4 2.2 fusion.31
  681.6 1.1 fusion.35
  682.8 0.3 fusion.33
  683.1 0.0 copy-done.3
  683.1 0.9 fusion.1
  684.0 0.0 copy-done.4
  684.0 0.4 fusion.11
  684.4 0.0 copy-done.7
  684.4 0.0 copy-start.1
  684.4 4.9 convolution_subtract_fusion.1
  689.3 0.0 copy-done.1
  689.3 3.4 fusion.13
  692.7 0.0 all-reduce.9.cloned.1.call-update
  692.7 0.3 all-reduce.11.cloned.1.call-start
  693.0 7.8 fusion.50
  700.8 76.0 %all-reduce.9.cloned.1.call-done = f32[448,128]{1,0:T(8,128)} async-done(((f32[448,128]{1,0:T(8,128)}), f32[448,128]{1,0:T(8,128)}) %all-reduce.9.cloned.1.call-update) | async-done | bytes 229392 | tf_op jit(solution)/shard_map/psum | solution.py:50
  776.8 2.3 convolution_bitcast_fusion.1
  779.0 0.0 all-reduce.11.cloned.1.call-update
  779.1 2.4 copy.8
  781.5 2.0 fusion.29
  783.5 227.6 %all-reduce.11.cloned.1.call-done = (f32[1792,128]{1,0:T(8,128)}, f32[128,128]{0,1:T(8,128)}) async-done(((f32[1792,128]{1,0:T(8,128)}, f32[128,128]{0,1:T(8,128)}), (f32[1792,128]{1,0:T(8,128)}, f32[128,128]{0,1:T(8,128)})) %all-reduce.11.cloned.1.call-update) | async-done | bytes 983056 | tf_op jit(solution)/shard_map/psum | solution.py:28
  1011.1 0.0 copy-start.5
  1011.1 0.0 copy-start.11
  1011.1 0.0 copy-start.6
  1011.1 0.0 copy-start.9
  1011.1 2.3 fusion.23
  1013.4 1.1 fusion.27
  1014.5 0.3 fusion.25
  1014.8 2.1 fusion
  1016.9 0.0 copy-done.5
  1016.9 0.0 copy-done.11
  1016.9 0.4 fusion.9
  1017.3 0.0 copy-done.6
  1017.3 0.0 copy-done.9
  1017.3 4.4 convolution_subtract_fusion
Async XLA Ops:
  14.5 325.5 %all-to-all-start = ((f32[32,2,448,128]{3,2,1,0:T(8,128)}), f32[32,2,448,128]{3,2,1,0:T(8,128)}, u32[]{:S(2)}, u32[]{:S(2)}) async-start(f32[32,2,448,128]{3,2,1,0:T(8,128)} %stack.2), calls=%async_computation | async-start | bytes 29360128 | tf_op jit(solution)/shard_map/all_to_all | solution.py:38
  25.7 419.3 %all-reduce.7.cloned.1.call-start = ((), (), s32[]{:S(2)}) async-start(), calls=%async_computation.1 | async-start | bytes 458752 | tf_op jit(solution)/shard_map/psum | solution.py:50
  352.0 3.6 copy-start
  354.7 0.9 copy-start.2
  359.0 320.4 %all-reduce.13.cloned.1.call-start = ((), (), s32[]{:S(2)}) async-start(), calls=%async_computation.4 | async-start | bytes 1966080 | tf_op jit(solution)/shard_map/psum | solution.py:28
  367.0 84.8 %copy-start.8 = (f32[2,128,128]{2,1,0:T(8,128)S(1)}, f32[2,128,128]{2,1,0:T(8,128)}, u32[]{:S(2)}) copy-start(f32[2,128,128]{2,1,0:T(8,128)} %param.5) | copy-start | bytes 393220
  445.0 6.9 copy-start.10
  447.3 235.8 %copy-start.3 = (f32[1,1792,128]{2,1,0:T(8,128)S(1)}, f32[1,1792,128]{2,1,0:T(8,128)}, u32[]{:S(2)}) copy-start(f32[1,1792,128]{2,1,0:T(8,128)} %copy-done.2) | copy-start | bytes 2752516
  447.3 329.5 %all-reduce.9.cloned.1.call-start = ((), (), s32[]{:S(2)}) async-start(), calls=%async_computation.2 | async-start | bytes 458752 | tf_op jit(solution)/shard_map/psum | solution.py:50
  451.9 232.2 %copy-start.4 = (f32[2,448,128]{2,1,0:T(8,128)S(1)}, f32[2,448,128]{2,1,0:T(8,128)}, u32[]{:S(2)}) copy-start(f32[2,448,128]{2,1,0:T(8,128)} %param.4) | copy-start | bytes 1376260
  679.4 5.0 copy-start.7
  684.4 4.9 copy-start.1
  692.7 318.4 %all-reduce.11.cloned.1.call-start = ((), (), s32[]{:S(2)}) async-start(), calls=%async_computation.3 | async-start | bytes 1966080 | tf_op jit(solution)/shard_map/psum | solution.py:28
  1011.1 5.8 copy-start.5
  1011.1 5.8 copy-start.11
  1011.1 6.2 copy-start.6
  1011.1 6.2 copy-start.9
Sparse Core Ops, SparseCore 0:
  359.1 85.7 all-reduce.6
  447.7 231.7 all-reduce.12
  692.8 83.8 all-reduce.8
  779.3 231.7 all-reduce.10

commit v2 on v0

--- a/solution.py
+++ b/solution.py
@@ -39,7 +39,9 @@
         vector_rows = panels[number]
         vcol_now = vector_cols[number]
         factor = factors[number]
-        forward = lax.psum(matmul(current, vcol_now), "col")
+        x = matmul(current, vcol_now)
+        parts = lax.all_gather(x, "col", axis=0, tiled=False)
+        forward = parts.sum(axis=0)
         forward_cols, summed = row_sums(
             current, vector_rows, (transposed_dot(vector_rows, forward),)
         )

time: 775 us -> 718 us (0.926)
  waiting for transfers between devices: 705 us -> 646 us
    psum x2 -> x0, waiting for transfers between devices: 151 us -> none  [shards(): forward = lax.psum(matmul(current, vcol_now), 'col')]
    all_gather x0 -> x2, waiting for transfers between devices: none -> 100 us  [shards(): parts = lax.all_gather(x, 'col', axis=0, tiled=False)]
    psum x2, waiting for transfers between devices: 459 us -> 450 us  [row_sums(): lax.psum((transposed_dot(current, vector_rows),) + extra_terms, 'row')]
where the time goes in v2:
time: 718 us; the launch traced here: 717 us
  waiting for transfers between devices  646 us (90%)
  matrix products  49.3 us (7%)
  between operations  13.3 us (2%)
    psum x2, waiting for transfers between devices, row_sums(): lax.psum((transposed_dot(current, vector_rows),) + extra_terms, 'row')  450 us
    all_gather x2, waiting for transfers between devices, shards(): parts = lax.all_gather(x, 'col', axis=0, tiled=False)  100 us
    all_gather x1, waiting for transfers between devices, shards(): gathered = lax.all_gather(panels, 'row', axis=1, tiled=True)  95.2 us
    dot_general x4, matrix products, transposed_dot(): lax.dot_general(former, latter, (((0,), (0,)), ((), ())), precision=lax.P...  19.9 us
    dot_general x14, matrix products, matmul(): return jnp.dot(former, latter, precision=lax.Precision.HIGHEST)  19.8 us
  transfers between devices with their start and end apart: 5, of which 5 were waited for; matrix products, arithmetic and copies ran while one was open for 3% of the time, Pallas kernels for 0%

profile of v2, /device:TPU:1, one launch (start us, length us, event | category | flops | bytes accessed | tf_op | source)
XLA Modules:
  0.0 717.4 jit_solution(3361767524532197473)
XLA Ops:
  6.5 0.0 copy-start
  6.5 0.0 all-gather.6.cloned.1.call-start
  6.5 0.7 all-gather.6.cloned.1.call-update
  7.3 0.0 all-gather.8.cloned.1.call-start
  7.3 95.2 %all-gather.6.cloned.1.call-done = f32[2,14336,128]{2,1,0:T(8,128)} async-done(((f32[2,448,128]{2,1,0:T(8,128)}), f32[2,14336,128]{2,1,0:T(8,128)}) %all-gather.6.cloned.1.call-update) | async-done | bytes 14680080 | tf_op jit(solution)/shard_map/all_gather | solution.py:35
  102.5 2.5 dynamic-slice_bitcast_fusion
  105.0 0.0 copy-start.3
  105.0 0.9 copy-done.3
  105.9 0.0 copy-done
  105.9 3.4 convolution_bitcast_fusion
  109.3 0.0 all-gather.8.cloned.1.call-update
  109.3 0.0 all-reduce.7.cloned.1.call-start
  109.4 7.8 %fusion.44 = f32[1792,128]{1,0:T(8,128)} fusion(f32[448,1792]{1,0:T(8,128)S(1)} %copy-done, f32[2,448,128]{2,1,0:T(8,128)} %param.4), kind=kOutput, calls=%fused_computation.57 | convolution fusion | flops 1233125376 | bytes 4358144 | tf_op jit(solution)/shard_map/dot_general | solution.py:12
  117.1 0.0 copy-start.5
  117.1 0.0 copy-start.7
  117.1 49.3 %all-gather.8.cloned.1.call-done = f32[3584,128]{1,0:T(8,128)} async-done(((f32[448,128]{1,0:T(8,128)}), f32[3584,128]{1,0:T(8,128)}) %all-gather.8.cloned.1.call-update) | async-done | bytes 1835024 | tf_op jit(solution)/shard_map/all_gather | solution.py:43
  166.4 0.0 copy-start.4
  166.4 1.7 reduce_sum.18
  168.1 2.2 convolution_bitcast_fusion.2
  170.3 0.0 all-reduce.7.cloned.1.call-update
  170.3 0.2 all-gather.10.cloned.1.call-start
  170.5 0.0 copy-done.5
  170.6 0.8 slice_bitcast_fusion
  171.4 0.0 copy-done.7
  171.4 0.3 fusion.32
  171.7 225.3 %all-reduce.7.cloned.1.call-done = (f32[1792,128]{1,0:T(8,128)}, f32[128,128]{0,1:T(8,128)}) async-done(((f32[1792,128]{1,0:T(8,128)}, f32[128,128]{0,1:T(8,128)}), (f32[1792,128]{1,0:T(8,128)}, f32[128,128]{0,1:T(8,128)})) %all-reduce.7.cloned.1.call-update) | async-done | bytes 983056 | tf_op jit(solution)/shard_map/psum | solution.py:28
  397.0 0.0 copy-start.9
  397.0 2.1 fusion.26
  399.1 1.1 fusion.30
  400.2 0.3 fusion.28
  400.5 0.0 copy-done.4
  400.5 0.9 fusion.1
  401.5 0.4 fusion.11
  401.8 0.0 copy-done.9
  401.8 0.0 copy-start.1
  401.8 5.1 convolution_subtract_fusion.1
  406.9 0.0 copy-done.1
  406.9 3.4 fusion.46
  410.3 0.0 all-gather.10.cloned.1.call-update
  410.3 0.3 all-reduce.5.cloned.1.call-start
  410.6 7.8 %fusion.45 = f32[1792,128]{1,0:T(8,128)} fusion(f32[448,1792]{1,0:T(8,128)S(1)} %convolution_subtract_fusion.1, f32[2,448,128]{2,1,0:T(8,128)} %param.4), kind=kOutput, calls=%fused_computation.58 | convolution fusion | flops 1233125376 | bytes 4358144 | tf_op jit(solution)/shard_map/dot_general | solution.py:12
  418.4 50.7 %all-gather.10.cloned.1.call-done = f32[3584,128]{1,0:T(8,128)} async-done(((f32[448,128]{1,0:T(8,128)}), f32[3584,128]{1,0:T(8,128)}) %all-gather.10.cloned.1.call-update) | async-done | bytes 1835024 | tf_op jit(solution)/shard_map/all_gather | solution.py:43
  469.0 2.3 reduce_sum.19
  471.3 2.3 convolution_bitcast_fusion.1
  473.6 0.0 all-reduce.5.cloned.1.call-update
  473.6 2.0 fusion.24
  475.6 224.7 %all-reduce.5.cloned.1.call-done = (f32[1792,128]{1,0:T(8,128)}, f32[128,128]{0,1:T(8,128)}) async-done(((f32[1792,128]{1,0:T(8,128)}, f32[128,128]{0,1:T(8,128)}), (f32[1792,128]{1,0:T(8,128)}, f32[128,128]{0,1:T(8,128)})) %all-reduce.5.cloned.1.call-update) | async-done | bytes 983056 | tf_op jit(solution)/shard_map/psum | solution.py:28
  700.3 0.0 copy-start.6
  700.3 0.0 copy-start.10
  700.3 0.0 copy-start.2
  700.3 0.0 copy-start.8
  700.3 2.2 fusion.18
  702.5 1.1 fusion.22
  703.6 0.3 fusion.20
  703.9 2.1 fusion
  706.0 0.0 copy-done.6
  706.0 0.0 copy-done.10
  706.0 0.4 fusion.9
  706.4 0.0 copy-done.2
  706.4 0.0 copy-done.8
  706.4 4.5 convolution_subtract_fusion
Async XLA Ops:
  6.5 99.4 %copy-start = (f32[448,1792]{1,0:T(8,128)S(1)}, f32[448,1792]{1,0:T(8,128)}, u32[]{:S(2)}) copy-start(f32[448,1792]{1,0:T(8,128)} %param.3) | copy-start | bytes 9633796
  6.5 96.0 %all-gather.6.cloned.1.call-start = ((), (), s32[]{:S(2)}) async-start(), calls=%async_computation | async-start | bytes 15138816 | tf_op jit(solution)/shard_map/all_gather | solution.py:35
  7.3 159.2 %all-gather.8.cloned.1.call-start = ((), (), s32[]{:S(2)}) async-start(), calls=%async_computation.1 | async-start | bytes 2064384 | tf_op jit(solution)/shard_map/all_gather | solution.py:43
  105.0 0.9 copy-start.3
  109.3 287.7 %all-reduce.7.cloned.1.call-start = ((), (), s32[]{:S(2)}) async-start(), calls=%async_computation.4 | async-start | bytes 1966080 | tf_op jit(solution)/shard_map/psum | solution.py:28
  117.1 53.4 %copy-start.5 = (f32[2,448,128]{2,1,0:T(8,128)S(1)}, f32[2,448,128]{2,1,0:T(8,128)}, u32[]{:S(2)}) copy-start(f32[2,448,128]{2,1,0:T(8,128)} %param.4) | copy-start | bytes 1376260
  117.1 54.2 %copy-start.7 = (f32[2,128,128]{2,1,0:T(8,128)S(1)}, f32[2,128,128]{2,1,0:T(8,128)}, u32[]{:S(2)}) copy-start(f32[2,128,128]{2,1,0:T(8,128)} %param.5) | copy-start | bytes 393220
  166.4 234.1 %copy-start.4 = (f32[1792,128]{1,0:T(8,128)S(1)}, f32[1792,128]{1,0:T(8,128)}, u32[]{:S(2)}) copy-start(f32[1792,128]{1,0:T(8,128)} %copy-done.3) | copy-start | bytes 2752516
  170.3 298.7 %all-gather.10.cloned.1.call-start = ((), (), s32[]{:S(2)}) async-start(), calls=%async_computation.2 | async-start | bytes 2064384 | tf_op jit(solution)/shard_map/all_gather | solution.py:43
  397.0 4.8 copy-start.9
  401.8 5.1 copy-start.1
  410.3 290.0 %all-reduce.5.cloned.1.call-start = ((), (), s32[]{:S(2)}) async-start(), calls=%async_computation.3 | async-start | bytes 1966080 | tf_op jit(solution)/shard_map/psum | solution.py:28
  700.3 5.7 copy-start.6
  700.3 5.7 copy-start.10
  700.3 6.1 copy-start.2
  700.3 6.1 copy-start.8
Sparse Core Ops, SparseCore 0:
  9.1 93.3 all-gather.5
  109.4 56.9 all-gather.7
  170.4 226.5 all-reduce.6
  410.5 58.5 all-gather.9
  473.7 226.5 all-reduce.4
